TPU v7x, 256 devices: a whole 4x4x8 slice. The times are simulated.
256 devices in a mesh: grp: 4 (over y), dom: 64 (over x, z, core).
Axes of the slice: x: 4, y: 4, z: 8, core: 2. Of those that a mesh axis runs over, the one named last changes fastest.
Arguments:
- features: bfloat16 [786432, 256], P(('grp', 'dom')), may hold values from -6 to 6
- boundary_cache: float32 [65536, 256], P(('grp', 'dom')), may hold values from -6 to 6
- adjacency: bfloat16 [6144, 2, 128, 128], P(('grp', 'dom')), may hold values from -0.375 to 0.375
- neighbor: int32 [6144, 2], P(('grp', 'dom')), may hold values from 0 to 87
- counts: int32 [6144], P(('grp', 'dom')), may hold values from 1 to 2
- wanted: int32 [256, 64], P(('grp', 'dom')), may hold values from 0 to 1
- weight_in: bfloat16 [512, 512], replicated, may hold values from -0.25 to 0.25
- weight_out: bfloat16 [512, 256], replicated, may hold values from -0.25 to 0.25
- cotangent: bfloat16 [786432, 256], P(('grp', 'dom')), may hold values from -6 to 6
Outputs:
- grad_features: bfloat16 [786432, 256], P(('grp', 'dom'))
- grad_weight_in: float32 [512, 512], P('dom')
- grad_weight_out: float32 [512, 256], P('dom')
Inputs may be any that keep to these rules, and one draw needn't show every extreme that they name: `neighbor`: A value under 24 names a block of the same partition; a value 24 + q names the boundary block that the partition reads from partition q of its group. Slots from counts[b] on are padding and carry no edges.
All inputs are finite; a program needn't handle non-finite values.
Results may differ from a plain program's by a relative error of at most 0.0054.
Values may be sent and summed in bfloat16 or wider, within the bound.
No kernel may reach another device: no remote copies, remote signals or barrier semaphores. Data moves between devices by JAX's collectives and lax.ppermute only.
A program may use at most 128 MiB of HBM per device.

v0:
```python
import math
import jax
import jax.numpy as jnp
from jax import lax
from jax.sharding import PartitionSpec as P


def local(
    features, boundary_cache, adjacency, neighbor, counts, wanted, weight_in, weight_out, cotangent
):
    nblocks = adjacency.shape[0]
    slot_total = adjacency.shape[1]
    block_rows = adjacency.shape[2]
    channels = features.shape[1]
    node_rows = nblocks * block_rows
    partners = lax.axis_size("dom")
    cache_copy = boundary_cache.astype(jnp.bfloat16)
    exported = cache_copy.reshape(-1, block_rows, channels)
    export_total = exported.shape[0]
    exported_all = lax.all_gather(cache_copy, "dom", axis=0, tiled=True).reshape(
        partners, export_total, block_rows, channels
    )
    selected = wanted[0]
    boundary = exported_all[:, 0]
    boundary = jnp.where((selected == 1)[:, None, None], exported_all[:, 1], boundary)
    owned = features.reshape(nblocks, block_rows, channels)
    sources = jnp.concatenate([owned, boundary], 0)
    active = jnp.arange(slot_total)[None, :] < counts[:, None]
    chosen = sources[neighbor]
    chosen = jnp.where(active[:, :, None, None], chosen, jnp.zeros_like(chosen))
    aggregate = jnp.einsum("bsij,bsjf->bif", adjacency, chosen, preferred_element_type=jnp.float32)
    aggregate = aggregate.astype(jnp.bfloat16).reshape(node_rows, channels)
    joined = jnp.concatenate([aggregate, features], 1)
    preact = jnp.dot(joined, weight_in, preferred_element_type=jnp.float32)
    gating = jax.nn.sigmoid(preact)
    hidden = (preact * gating).astype(jnp.bfloat16)
    grad_hidden = jnp.einsum("nf,hf->nh", cotangent, weight_out, preferred_element_type=jnp.float32)
    grad_preact = (grad_hidden * gating * (1.0 + preact * (1.0 - gating))).astype(jnp.bfloat16)
    grad_joined = jnp.einsum(
        "nh,ch->nc", grad_preact, weight_in, preferred_element_type=jnp.float32
    )
    grad_aggregate = (
        grad_joined[:, :channels].astype(jnp.bfloat16).reshape(nblocks, block_rows, channels)
    )
    backward = jnp.einsum(
        "bsji,bjf->bsif", adjacency, grad_aggregate, preferred_element_type=jnp.float32
    )
    local_hit = active & (neighbor < nblocks)
    routing = (neighbor[None, :, :] == jnp.arange(nblocks)[:, None, None]) & local_hit[None]
    spread = jnp.einsum(
        "cbs,bsif->cif", routing.astype(jnp.float32), backward, precision=lax.Precision.HIGHEST
    )
    grad_features = (grad_joined[:, channels:] + spread.reshape(node_rows, channels)).astype(
        jnp.bfloat16
    )
    node_total = node_rows * lax.axis_size("grp") * partners
    loss_scale = 1.0 / math.sqrt(node_total)
    rows_in = weight_in.shape[0] // partners
    rows_out = weight_out.shape[0] // partners
    summed = lax.psum(
        (
            jnp.einsum("nc,nh->ch", joined, grad_preact, preferred_element_type=jnp.float32)
            * loss_scale,
            jnp.einsum("nh,nf->hf", hidden, cotangent, preferred_element_type=jnp.float32)
            * loss_scale,
        ),
        ("grp", "dom"),
    )
    position = lax.axis_index("dom")
    grad_weight_in = lax.dynamic_slice_in_dim(summed[0], position * rows_in, rows_in, 0)
    grad_weight_out = lax.dynamic_slice_in_dim(summed[1], position * rows_out, rows_out, 0)
    return (grad_features, grad_weight_in, grad_weight_out)


def solution(mesh):
    in_specs = (
        P(("grp", "dom"), None),
        P(("grp", "dom"), None),
        P(("grp", "dom"), None, None, None),
        P(("grp", "dom"), None),
        P(("grp", "dom")),
        P(("grp", "dom"), None),
        P(),
        P(),
        P(("grp", "dom"), None),
    )
    out_specs = (P(("grp", "dom"), None), P("dom", None), P("dom", None))
    return jax.shard_map(local, mesh=mesh, in_specs=in_specs, out_specs=out_specs, check_vma=False)
```

profile of v0, /device:TPU:2, one launch (start us, length us, event | category | flops | bytes accessed | tf_op | source)
XLA Modules:
  0.0 416.0 jit_solution(14826898906315317452)
XLA Ops:
  7.2 0.0 copy-start
  7.2 0.0 all-gather.2.cloned.1.call-start
  7.2 1.7 convert_element_type.20
  9.0 0.0 all-gather.2.cloned.1.call-update
  9.0 0.0 all-reduce.3.cloned.1.call-start
  9.0 0.7 compare_and_fusion
  9.7 0.1 copy.16
  9.8 0.7 compare_select_fusion
  10.5 0.1 copy.18
  10.6 0.1 reshape.58
  10.7 0.7 compare_bitcast_fusion
  11.4 84.6 %all-gather.2.cloned.1.call-done = bf16[16384,256]{1,0:T(8,128)(2,1)} async-done(((bf16[256,256]{1,0:T(8,128)(2,1)}), bf16[16384,256]{1,0:T(8,128)(2,1)}) %all-gather.2.cloned.1.call-update) | async-done | bytes 8388624 | tf_op jit(solution)/shard_map/all_gather | solution.py:20
  96.0 0.0 copy-start.3
  96.0 3.9 fusion.2
  99.9 0.0 copy-done.3
  99.9 3.0 pad_maximum_fusion
  102.9 5.2 %gather_fusion = bf16[48,128,256]{2,1,0:T(8,128)(2,1)} fusion(bf16[88,128,256]{2,1,0:T(8,128)(2,1)} %pad_maximum_fusion, s32[1024]{0:T(1024)S(1)} %pad_clamp_fusion), kind=kCustom, calls=%fused_computation | custom fusion | bytes 6291648 | tf_op jit(solution)/shard_map/gather | solution.py:29
  108.1 0.0 copy-done
  108.1 0.0 copy-start.4
  108.1 2.6 bitcast_convert_fusion
  110.8 0.0 copy-done.4
  110.8 0.0 copy-start.6
  110.8 1.8 fusion.9
  112.6 0.0 copy-done.6
  112.6 0.0 copy-start.7
  112.6 2.6 fusion.17
  115.2 0.0 copy-done.7
  115.2 2.7 multiply_convert_fusion.1
  118.0 0.0 copy-start.2
  118.0 1.6 copy-done.2
  119.6 2.8 fusion.16
  122.4 3.8 fusion.27
  126.2 0.0 copy-start.1
  126.2 2.6 copy-done.1
  128.8 0.2 slice.33
  129.0 3.7 fusion.28
  132.7 0.0 copy-start.5
  132.7 6.6 %copy.22 = f32[24,256,2,128]{1,0,2,3:T(8,128)} copy(f32[24,256,2,128]{3,1,2,0:T(8,128)} %fusion.28) | data formatting | bytes 12582912 | tf_op jit(solution)/shard_map/bsji,bjf->bsif/dot_general | solution.py:45
  139.4 0.0 copy-done.5
  139.4 4.4 %fusion.10 = f32[24,128,256]{2,0,1:T(8,128)S(1)} fusion(f32[24,256,2,128]{1,0,2,3:T(8,128)} %copy.22, s32[24,2]{0,1:T(2,128)S(1)} %copy-done.5, pred[24,2]{0,1:T(4,128)(4,1)S(1)} %get-tuple-element.5), kind=kOutput, calls=%fused_computation.21 | convolution fusion | flops 452987136 | bytes 9437424 | tf_op jit(solution)/shard_map/cbs,bsif->cif/dot_general | solution.py:50
  143.8 2.7 copy.19
  146.5 0.0 all-reduce.3.cloned.1.call-update
  146.5 4.3 %fusion.3 = bf16[3072,256]{1,0:T(8,128)(2,1)} fusion(f32[3072,512]{1,0:T(8,128)} %copy-done.1, f32[24,128,256]{2,1,0:T(8,128)} %copy.19), kind=kLoop, calls=%fused_computation.12 | loop fusion | flops 1572864 | bytes 7864320 | tf_op jit(solution)/shard_map/convert_element_type | solution.py:53
  150.8 255.8 %all-reduce.3.cloned.1.call-done = (f32[512,512]{1,0:T(8,128)}, f32[512,256]{1,0:T(8,128)}) async-done(((f32[512,512]{1,0:T(8,128)}, f32[512,256]{1,0:T(8,128)}), (f32[512,512]{1,0:T(8,128)}, f32[512,256]{1,0:T(8,128)})) %all-reduce.3.cloned.1.call-update) | async-done | bytes 1572880 | tf_op jit(solution)/shard_map/psum | solution.py:60
  406.6 1.3 constant_dynamic-slice_fusion.1
  407.9 1.3 constant_dynamic-slice_fusion
  (1 shorter events, 0.0 us)
Async XLA Ops:
  7.2 101.0 %copy-start = (bf16[24,2,128,128]{3,2,1,0:T(8,128)(2,1)S(1)}, bf16[24,2,128,128]{3,2,1,0:T(8,128)(2,1)}, u32[]{:S(2)}) copy-start(bf16[24,2,128,128]{3,2,1,0:T(8,128)(2,1)} %param.11) | copy-start | bytes 4718596
  7.2 88.8 %all-gather.2.cloned.1.call-start = ((), (), s32[]{:S(2)}) async-start(), calls=%async_computation | async-start | bytes 8519680 | tf_op jit(solution)/shard_map/all_gather | solution.py:20
  9.0 397.6 %all-reduce.3.cloned.1.call-start = ((), (), s32[]{:S(2)}) async-start(), calls=%async_computation.1 | async-start | bytes 3145728 | tf_op jit(solution)/shard_map/psum | solution.py:60
  96.0 3.9 copy-start.3
  108.1 2.6 copy-start.4
  110.8 1.8 copy-start.6
  112.6 2.6 copy-start.7
  118.0 1.6 copy-start.2
  126.2 2.6 copy-start.1
  132.7 6.6 %copy-start.5 = (s32[24,2]{0,1:T(2,128)S(1)}, s32[24,2]{0,1:T(2,128)}, u32[]{:S(2)}) copy-start(s32[24,2]{0,1:T(2,128)} %param.12) | copy-start | bytes 580
Sparse Core Ops, SparseCore 0:
  11.3 84.6 all-gather.1
  146.6 259.9 all-reduce.2
where the time goes:
time: 416 us
  waiting for transfers between devices  340 us (82%)
  matrix products  24.4 us (6%)
  local copies, waits for them, and re-layouts  21.9 us (5%)
  other arithmetic  15 us (4%)
  between operations  14.2 us (3%)
    psum x1, waiting for transfers between devices, local(): lax.psum((jnp.einsum('nc,nh->ch', joined, grad_preact, preferred_element_...  256 us
    all_gather x1, waiting for transfers between devices, local(): lax.all_gather(cache_copy, 'dom', axis=0, tiled=True)  84.6 us
  transfers between devices with their start and end apart: 2, of which 2 were waited for; matrix products, arithmetic and copies ran while one was open for 2% of the time, Pallas kernels for 0%

commit v1 on v0

--- a/solution.py
+++ b/solution.py
@@ -3,6 +3,8 @@
 import jax.numpy as jnp
 from jax import lax
 from jax.sharding import PartitionSpec as P
+
+_search_roots = lambda local_block: lax.psum(lax.psum(local_block, "dom"), "grp")
 
 
 def local(
@@ -57,14 +59,13 @@
     loss_scale = 1.0 / math.sqrt(node_total)
     rows_in = weight_in.shape[0] // partners
     rows_out = weight_out.shape[0] // partners
-    summed = lax.psum(
+    summed = _search_roots(
         (
             jnp.einsum("nc,nh->ch", joined, grad_preact, preferred_element_type=jnp.float32)
             * loss_scale,
             jnp.einsum("nh,nf->hf", hidden, cotangent, preferred_element_type=jnp.float32)
             * loss_scale,
-        ),
-        ("grp", "dom"),
+        )
     )
     position = lax.axis_index("dom")
     grad_weight_in = lax.dynamic_slice_in_dim(summed[0], position * rows_in, rows_in, 0)

time: 416 us -> 377 us (0.906)
  waiting for transfers between devices: 340 us -> 303 us
    psum x1 -> x2, waiting for transfers between devices: 256 us -> 219 us  [the longest x1 181 us: lax.psum(local_block, 'dom')]
  transfers between devices with their start and end apart: 2 -> 3, of which waited for: 2 -> 3; matrix products, arithmetic and copies ran while one was open for 2% -> 7% of each run, Pallas kernels for 0% -> 0%
where the time goes in v1:
time: 377 us; the launch traced here: 376 us
  waiting for transfers between devices  303 us (80%)
  matrix products  24.4 us (6%)
  local copies, waits for them, and re-layouts  20.4 us (5%)
  other arithmetic  14.1 us (4%)
  between operations  13.9 us (4%)
    psum x1, waiting for transfers between devices, lax.psum(local_block, 'dom')  181 us
    all_gather x1, waiting for transfers between devices, local(): lax.all_gather(cache_copy, 'dom', axis=0, tiled=True)  84.7 us
    psum x1, waiting for transfers between devices, lax.psum(lax.psum(local_block, 'dom'), 'grp')  37.9 us
  transfers between devices with their start and end apart: 3, of which 3 were waited for; matrix products, arithmetic and copies ran while one was open for 7% of the time, Pallas kernels for 0%

profile of v1, /device:TPU:2, one launch (start us, length us, event | category | flops | bytes accessed | tf_op | source)
XLA Modules:
  0.0 376.3 jit_solution(17169981892298824667)
XLA Ops:
  7.2 0.0 copy-start
  7.2 0.0 all-gather.2.cloned.1.call-start
  7.2 1.7 convert_element_type.20
  9.0 0.0 all-gather.2.cloned.1.call-update
  9.0 0.0 all-reduce.5.cloned.1.call-start
  9.0 0.7 compare_and_fusion
  9.7 0.1 copy.16
  9.8 0.7 compare_select_fusion
  10.5 0.1 copy.18
  10.6 0.1 reshape.58
  10.7 0.7 compare_bitcast_fusion
  11.4 84.7 %all-gather.2.cloned.1.call-done = bf16[16384,256]{1,0:T(8,128)(2,1)} async-done(((bf16[256,256]{1,0:T(8,128)(2,1)}), bf16[16384,256]{1,0:T(8,128)(2,1)}) %all-gather.2.cloned.1.call-update) | async-done | bytes 8388624 | tf_op jit(solution)/shard_map/all_gather | solution.py:22
  96.0 0.0 copy-start.3
  96.0 3.9 %fusion.2 = bf16[64,128,256]{2,1,0:T(8,128)(2,1)S(1)} fusion(bf16[64,2,128,256]{3,2,1,0:T(8,128)(2,1)} %bitcast.49, pred[64]{0:T(512)(128)(4,1)S(1)} %compare_bitcast_fusion), kind=kLoop, calls=%fused_computation.8 | loop fusion | flops 2097152 | bytes 12582976 | tf_op jit(solution)/shard_map/jit(_where)/select_n | solution.py:27
  99.9 0.0 copy-done.3
  99.9 3.0 pad_maximum_fusion
  102.9 5.2 %gather_fusion = bf16[48,128,256]{2,1,0:T(8,128)(2,1)} fusion(bf16[88,128,256]{2,1,0:T(8,128)(2,1)} %pad_maximum_fusion, s32[1024]{0:T(1024)S(1)} %pad_clamp_fusion), kind=kCustom, calls=%fused_computation | custom fusion | bytes 6291648 | tf_op jit(solution)/shard_map/gather | solution.py:31
  108.1 0.0 copy-done
  108.1 0.0 copy-start.4
  108.1 2.6 bitcast_convert_fusion
  110.8 0.0 copy-done.4
  110.8 0.0 copy-start.6
  110.8 1.8 fusion.9
  112.6 0.0 copy-done.6
  112.6 0.0 copy-start.7
  112.6 2.6 fusion.17
  115.2 0.0 copy-done.7
  115.2 2.7 multiply_convert_fusion.1
  117.9 0.0 copy-start.2
  118.0 1.6 copy-done.2
  119.6 2.8 fusion.16
  122.4 0.0 all-reduce.5.cloned.1.call-update
  122.4 0.2 all-reduce.7.cloned.1.call-start
  122.6 3.8 %fusion.27 = f32[3072,512]{1,0:T(8,128)S(1)} fusion(bf16[3072,512]{1,0:T(8,128)(2,1)} %copy-done.2, bf16[512,512]{1,0:T(8,128)(2,1)} %param.15), kind=kOutput, calls=%fused_computation.41 | convolution fusion | flops 1610612736 | bytes 9961472 | tf_op jit(solution)/shard_map/nh,ch->nc/dot_general | solution.py:41
  126.5 0.0 copy-start.1
  126.5 2.7 copy-done.1
  129.1 0.2 slice.33
  129.3 180.6 %all-reduce.5.cloned.1.call-done = (f32[512,512]{1,0:T(8,128)}, f32[512,256]{1,0:T(8,128)}) async-done(((f32[512,512]{1,0:T(8,128)}, f32[512,256]{1,0:T(8,128)}), (f32[512,512]{1,0:T(8,128)}, f32[512,256]{1,0:T(8,128)})) %all-reduce.5.cloned.1.call-update) | async-done | bytes 1572880 | tf_op jit(solution)/shard_map/psum | solution.py:7
  310.0 0.0 all-reduce.7.cloned.1.call-update
  310.0 3.7 fusion.28
  313.6 6.7 %copy.22 = f32[24,256,2,128]{1,0,2,3:T(8,128)} copy(f32[24,256,2,128]{3,1,2,0:T(8,128)} %fusion.28) | data formatting | bytes 12582912 | tf_op jit(solution)/shard_map/bsji,bjf->bsif/dot_general | solution.py:47
  320.4 0.0 copy-done.5
  320.4 4.4 %fusion.10 = f32[24,128,256]{2,0,1:T(8,128)S(1)} fusion(f32[24,256,2,128]{1,0,2,3:T(8,128)} %copy.22, s32[24,2]{0,1:T(2,128)S(1)} %copy-done.5, pred[24,2]{0,1:T(4,128)(4,1)S(1)} %get-tuple-element.7), kind=kOutput, calls=%fused_computation.21 | convolution fusion | flops 452987136 | bytes 9437424 | tf_op jit(solution)/shard_map/cbs,bsif->cif/dot_general | solution.py:52
  324.8 1.0 copy.19
  325.8 3.5 fusion.3
  329.3 37.9 %all-reduce.7.cloned.1.call-done = (f32[512,512]{1,0:T(8,128)}, f32[512,256]{1,0:T(8,128)}) async-done(((f32[512,512]{1,0:T(8,128)}, f32[512,256]{1,0:T(8,128)}), (f32[512,512]{1,0:T(8,128)}, f32[512,256]{1,0:T(8,128)})) %all-reduce.7.cloned.1.call-update) | async-done | bytes 1572880 | tf_op jit(solution)/shard_map/psum | solution.py:7
  367.2 1.3 constant_dynamic-slice_fusion.1
  368.5 1.3 constant_dynamic-slice_fusion
  (2 shorter events, 0.0 us)
Async XLA Ops:
  7.2 101.0 %copy-start = (bf16[24,2,128,128]{3,2,1,0:T(8,128)(2,1)S(1)}, bf16[24,2,128,128]{3,2,1,0:T(8,128)(2,1)}, u32[]{:S(2)}) copy-start(bf16[24,2,128,128]{3,2,1,0:T(8,128)(2,1)} %param.11) | copy-start | bytes 4718596
  7.2 88.8 %all-gather.2.cloned.1.call-start = ((), (), s32[]{:S(2)}) async-start(), calls=%async_computation | async-start | bytes 8519680 | tf_op jit(solution)/shard_map/all_gather | solution.py:22
  9.0 301.0 %all-reduce.5.cloned.1.call-start = ((), (), s32[]{:S(2)}) async-start(), calls=%async_computation.1 | async-start | bytes 3145728 | tf_op jit(solution)/shard_map/psum | solution.py:7
  96.0 3.9 %copy-start.3 = (bf16[3072,256]{1,0:T(8,128)(2,1)S(1)}, bf16[3072,256]{1,0:T(8,128)(2,1)}, u32[]{:S(2)}) copy-start(bf16[3072,256]{1,0:T(8,128)(2,1)} %param.9) | copy-start | bytes 4718596
  108.1 2.6 copy-start.4
  110.8 1.8 copy-start.6
  112.6 2.6 copy-start.7
  117.9 1.7 copy-start.2
  122.4 244.7 %all-reduce.7.cloned.1.call-start = ((), (), s32[]{:S(2)}) async-start(), calls=%async_computation.2 | async-start | bytes 3145728 | tf_op jit(solution)/shard_map/psum | solution.py:7
  126.5 2.7 copy-start.1
  313.6 6.7 %copy-start.5 = (s32[24,2]{0,1:T(2,128)S(1)}, s32[24,2]{0,1:T(2,128)}, u32[]{:S(2)}) copy-start(s32[24,2]{0,1:T(2,128)} %param.12) | copy-start | bytes 580
Sparse Core Ops, SparseCore 0:
  11.3 84.6 all-gather.1
  122.5 187.3 all-reduce.4
  312.5 54.6 all-reduce.6
